TPU v7x, 32 devices: a whole 2x2x4 slice. The times are simulated.
32 devices in a mesh: seq: 8 (over z, x), tier: 4 (over y, core).
Axes of the slice: x: 2, y: 2, z: 4, core: 2. Of those that a mesh axis runs over, the one named last changes fastest.
Arguments:
- layer_input: bfloat16 [8, 512, 1024], P('seq', 'tier'), may hold values from -6 to 6
- memory: bfloat16 [8, 512, 1024], P('seq', 'tier'), may hold values from -6 to 6
- compressed: bfloat16 [8, 512, 1024], P('seq', 'tier'), may hold values from -6 to 6
- seg_len: int32 [8], P('seq'), may hold values from 1 to 512, as said below
- hist_len: int32 [8], P('seq'), may hold values from 0 to 1024, as said below
- query_weight: bfloat16 [1024, 1024], replicated, may hold values from -0.1875 to 0.1875
- key_weight: bfloat16 [1024, 1024], replicated, may hold values from -0.1875 to 0.1875
- value_weight: bfloat16 [1024, 1024], replicated, may hold values from -0.1875 to 0.1875
- attn_out_weight: bfloat16 [1024, 1024], replicated, may hold values from -1 to 1
- ffn_in_weight: bfloat16 [1024, 4096], replicated, may hold values from -0.1875 to 0.1875
- ffn_out_weight: bfloat16 [4096, 1024], replicated, may hold values from -0.09375 to 0.09375
- norm_gain: float32 [1024], replicated, may hold values from 0.1 to 1.9
- head_slope: float32 [8], replicated, may hold values from 0.0005 to 0.05
- comp_weight: bfloat16 [3072, 1024], replicated, may hold values from -0.109375 to 0.109375
- cotangent: bfloat16 [8, 512, 1024], P('seq', 'tier'), may hold values from -6 to 6
Outputs:
- output: bfloat16 [8, 512, 1024], P('seq', 'tier')
- grad_input: float32 [8, 512, 1024], P('seq', 'tier')
- new_memory: bfloat16 [8, 512, 1024], P('seq', 'tier')
- new_compressed: bfloat16 [8, 512, 1024], P('seq', 'tier')
- grad_query_weight: float32 [1024, 1024], P('seq', 'tier')
- grad_key_weight: float32 [1024, 1024], P('seq', 'tier')
- grad_value_weight: float32 [1024, 1024], P('seq', 'tier')
- grad_attn_out_weight: float32 [1024, 1024], P('seq', 'tier')
- grad_ffn_in_weight: float32 [1024, 4096], P('seq', 'tier')
- grad_ffn_out_weight: float32 [4096, 1024], P('seq', 'tier')
- grad_comp_weight: float32 [3072, 1024], P('seq', 'tier')
- grad_norm_gain: float32 [1024], replicated
- grad_head_slope: float32 [8], replicated
Inputs may be any that keep to these rules, and one draw needn't show every extreme that they name: `seg_len`: the first sequence's segment is full; others may end early, as the last segment of a book does. `hist_len`: the first sequence has a full history; a book's early segments have a short one.
All inputs are finite; a program needn't handle non-finite values.
Results may differ from a plain program's by a relative error of at most 0.014.
Values may be sent and summed in bfloat16 or wider, within the bound.
A program may use at most 256 MiB of HBM per device.

v0:
```python
import math
import jax
import jax.numpy as jnp
from jax import lax
from jax.sharding import PartitionSpec as P

norm_eps = 1e-05
neg_large = -1e30
f32 = jnp.float32
bf16 = jnp.bfloat16


def gelu_tanh(values_in):
    return jax.nn.gelu(values_in, approximate=True)


def layer_norm(residual, norm_gain):
    centre = jnp.mean(residual, axis=-1, keepdims=True)
    deviation = residual - centre
    variance = jnp.mean(deviation * deviation, axis=-1, keepdims=True)
    return deviation * lax.rsqrt(variance + norm_eps) * norm_gain


def softmax_grad(weights, grad_weights):
    inner_sum = jnp.sum(weights * grad_weights, axis=-1, keepdims=True)
    return (weights * (grad_weights - inner_sum)).astype(bf16)


def mm(left, right):
    return jnp.dot(left, right, preferred_element_type=f32)


def mm_tn(left, right):
    return lax.dot_general(left, right, (((0,), (0,)), ((), ())), preferred_element_type=f32)


def mm_nt(left, right):
    return lax.dot_general(left, right, (((1,), (1,)), ((), ())), preferred_element_type=f32)


def per_device(
    layer_input,
    memory,
    compressed,
    seg_len,
    hist_len,
    query_weight,
    key_weight,
    value_weight,
    attn_out_weight,
    ffn_in_weight,
    ffn_out_weight,
    norm_gain,
    head_slope,
    comp_weight,
    cotangent,
):
    _, row_count, width = layer_input.shape
    tiers = lax.axis_size("tier")
    seqs = lax.axis_size("seq")
    tier_pos = lax.axis_index("tier")
    heads = head_slope.shape[0]
    head_dim = width // heads
    hpt = heads // tiers
    cb = hpt * head_dim
    ff = ffn_in_weight.shape[1]
    ffb = ff // tiers
    seg = row_count * tiers
    keys_n = 3 * seg
    ncomp = (seg + 2) // 3
    inv_root = 1.0 / math.sqrt(head_dim)
    length = seg_len[0]
    history = hist_len[0]
    own_ids = tier_pos * row_count + jnp.arange(row_count, dtype=jnp.int32)
    mask_own = (own_ids < length).astype(f32)[:, None]
    all_ids = jnp.arange(seg, dtype=jnp.int32)
    mask_all = (all_ids < length).astype(f32)[:, None]
    hidden_own = (layer_input[0].astype(f32) * mask_own).astype(bf16)
    raw_local = jnp.stack([compressed[0], memory[0], hidden_own], axis=0)
    raw_seq = lax.all_gather(raw_local, "tier", axis=1, tiled=True)
    cot_seq = lax.all_gather(cotangent[0], "tier", axis=0, tiled=True)
    context = raw_seq.reshape(keys_n, width)
    comp_rows = raw_seq[0]
    memory_rows = raw_seq[1]
    hidden_seq = raw_seq[2]
    col0 = tier_pos * cb
    wq_t = lax.dynamic_slice_in_dim(query_weight, col0, cb, axis=1)
    wk_t = lax.dynamic_slice_in_dim(key_weight, col0, cb, axis=1)
    wv_t = lax.dynamic_slice_in_dim(value_weight, col0, cb, axis=1)
    wkv_t = jnp.concatenate([wk_t, wv_t], axis=1)
    slope_t = lax.dynamic_slice_in_dim(head_slope, tier_pos * hpt, hpt)
    q_t = mm(hidden_seq, wq_t).astype(bf16)
    kv_t = mm(context, wkv_t).astype(bf16)
    q_h = q_t.reshape(seg, hpt, head_dim)
    k_h = kv_t[:, :cb].reshape(keys_n, hpt, head_dim)
    v_h = kv_t[:, cb:].reshape(keys_n, hpt, head_dim)
    key_ids = jnp.arange(keys_n, dtype=jnp.int32)
    offsets = (2 * seg + all_ids)[:, None] - key_ids[None, :]
    distance = offsets.astype(f32)
    in_history = (key_ids[None, :] < 2 * seg) & (key_ids[None, :] >= 2 * seg - history)
    in_segment = (key_ids[None, :] >= 2 * seg) & (offsets >= 0)
    key_valid = (in_history | in_segment)[None]
    scores = jnp.einsum("rhd,khd->hrk", q_h, k_h, preferred_element_type=f32) * inv_root
    scores = scores - slope_t[:, None, None] * distance[None]
    masked = jnp.where(key_valid, scores, neg_large)
    log_total = jax.nn.logsumexp(masked, axis=-1, keepdims=True)
    probs = jnp.exp(masked - log_total)
    probs_low = probs.astype(bf16)
    attended_t = jnp.einsum("hrk,khd->rhd", probs_low, v_h, preferred_element_type=f32)
    attended_t = attended_t.reshape(seg, cb).astype(bf16)
    attended = lax.all_to_all(attended_t, "tier", 0, 1, tiled=True)
    mem_k = k_h[seg : 2 * seg]
    mem_v = v_h[seg : 2 * seg]
    mem_scores = jnp.einsum("rhd,khd->hrk", q_h, mem_k, preferred_element_type=f32) * inv_root
    mem_probs = jax.nn.softmax(mem_scores, axis=-1).astype(bf16)
    from_memory = jnp.einsum("hrk,khd->rhd", mem_probs, mem_v, preferred_element_type=f32)
    padded = jnp.pad(memory_rows, ((0, 3 * ncomp - seg), (0, 0)))
    windows = padded.reshape(ncomp, 3 * width)
    comp_new = mm(windows, comp_weight).astype(bf16)
    ckv_t = mm(comp_new, wkv_t).astype(bf16)
    comp_k = ckv_t[:, :cb].reshape(ncomp, hpt, head_dim)
    comp_v = ckv_t[:, cb:].reshape(ncomp, hpt, head_dim)
    comp_scores = jnp.einsum("rhd,khd->hrk", q_h, comp_k, preferred_element_type=f32) * inv_root
    comp_probs = jax.nn.softmax(comp_scores, axis=-1)
    comp_low = comp_probs.astype(bf16)
    from_comp = jnp.einsum("hrk,khd->rhd", comp_low, comp_v, preferred_element_type=f32)
    grad_fc = ((from_comp - from_memory) * mask_all[:, :, None]).astype(bf16)
    grad_cw = jnp.einsum("rhd,khd->hrk", grad_fc, comp_v, preferred_element_type=f32)
    grad_cs = softmax_grad(comp_probs, grad_cw)
    grad_ck = (
        jnp.einsum("hrk,rhd->khd", grad_cs, q_h, preferred_element_type=f32) * inv_root
    ).astype(bf16)
    grad_cv = jnp.einsum("hrk,rhd->khd", comp_low, grad_fc, preferred_element_type=f32).astype(bf16)
    grad_ckv = jnp.concatenate([grad_ck.reshape(ncomp, cb), grad_cv.reshape(ncomp, cb)], axis=1)
    grad_comp_part = mm_nt(grad_ckv, wkv_t)
    grad_comp_t = lax.psum_scatter(grad_comp_part, "tier", scatter_dimension=1, tiled=True)
    grad_comp_t = grad_comp_t.astype(bf16)
    part_comp = mm_tn(windows, grad_comp_t)
    full_comp = jnp.concatenate([comp_rows[ncomp:], comp_new[:ncomp]], axis=0)
    new_compressed = lax.dynamic_slice_in_dim(full_comp, tier_pos * row_count, row_count, axis=0)
    hidden_f = hidden_own.astype(f32)
    residual = hidden_f + mm(attended, attn_out_weight)
    normed, norm_pull = jax.vjp(layer_norm, residual, norm_gain)
    normed_low = normed.astype(bf16)
    pre_act = mm(normed_low, ffn_in_weight)
    act_value, gelu_pull = jax.vjp(gelu_tanh, pre_act)
    activation = act_value.astype(bf16)
    ffn_result = mm(activation, ffn_out_weight)
    output = ((residual + ffn_result) * mask_own).astype(bf16)
    grad_rows = cotangent[0].astype(f32) * mask_own
    grad_low = grad_rows.astype(bf16)
    grad_act = mm_nt(grad_low, ffn_out_weight)
    grad_pre = gelu_pull(grad_act)[0].astype(bf16)
    grad_normed = mm_nt(grad_pre, ffn_in_weight)
    grad_resid_norm, part_gain = norm_pull(grad_normed)
    grad_resid = grad_rows + grad_resid_norm
    grad_att = grad_resid.astype(bf16)
    grad_attended = mm_nt(grad_att, attn_out_weight).astype(bf16)
    back_t = lax.all_to_all(jnp.stack([grad_attended, grad_att], axis=0), "tier", 2, 1, tiled=True)
    grad_attended_t = back_t[0]
    grad_att_t = back_t[1]
    fwd_seq = lax.all_gather(jnp.stack([normed_low, attended], axis=0), "tier", axis=1, tiled=True)
    normed_seq = fwd_seq[0]
    attended_seq = fwd_seq[1]
    grad_seq = (cot_seq.astype(f32) * mask_all).astype(bf16)
    pre_seq = mm(normed_seq, ffn_in_weight)
    act_seq = gelu_tanh(pre_seq).astype(bf16)
    fcol0 = tier_pos * ffb
    pre_seq_t = lax.dynamic_slice_in_dim(pre_seq, fcol0, ffb, axis=1)
    wfo_t = lax.dynamic_slice_in_dim(ffn_out_weight, fcol0, ffb, axis=0)
    grad_act_seq_t = mm_nt(grad_seq, wfo_t)
    _, gelu_pull_seq = jax.vjp(gelu_tanh, pre_seq_t)
    grad_pre_seq_t = gelu_pull_seq(grad_act_seq_t)[0].astype(bf16)
    grad_seq_t = lax.dynamic_slice_in_dim(grad_seq, col0, cb, axis=1)
    part_ffn_in = mm_tn(normed_seq, grad_pre_seq_t)
    part_ffn_out = mm_tn(act_seq, grad_seq_t)
    part_attn_out = mm_tn(attended_seq, grad_att_t)
    grad_att_h = grad_attended_t.reshape(seg, hpt, head_dim)
    grad_probs = jnp.einsum("rhd,khd->hrk", grad_att_h, v_h, preferred_element_type=f32)
    grad_scores = softmax_grad(probs, grad_probs)
    part_slope = -jnp.einsum("hrk,rk->h", grad_scores.astype(f32), distance)
    grad_q = (
        (jnp.einsum("hrk,khd->rhd", grad_scores, k_h, preferred_element_type=f32) * inv_root)
        .reshape(seg, cb)
        .astype(bf16)
    )
    grad_k = (
        (jnp.einsum("hrk,rhd->khd", grad_scores, q_h, preferred_element_type=f32) * inv_root)
        .reshape(keys_n, cb)
        .astype(bf16)
    )
    grad_v = jnp.einsum("hrk,rhd->khd", probs_low, grad_att_h, preferred_element_type=f32)
    grad_v = grad_v.reshape(keys_n, cb).astype(bf16)
    part_query = mm_tn(hidden_seq, grad_q)
    part_key = mm_tn(context, grad_k)
    part_value = mm_tn(context, grad_v)
    seg_grads = jnp.stack([grad_q, grad_k[2 * seg :], grad_v[2 * seg :]], axis=0)
    own_grads = lax.all_to_all(seg_grads, "tier", 1, 2, tiled=True)
    grad_hidden = grad_resid + mm_nt(own_grads[0], query_weight)
    grad_hidden = grad_hidden + mm_nt(own_grads[1], key_weight)
    grad_hidden = grad_hidden + mm_nt(own_grads[2], value_weight)
    grad_input = grad_hidden * mask_own
    parts = (part_query, part_key, part_value, part_attn_out, part_ffn_in, part_ffn_out, part_comp)
    flat = jnp.concatenate([p.reshape(seqs, -1, width) for p in parts], axis=1)
    flat = flat.reshape(-1, width)
    reduced = lax.psum_scatter(flat, "seq", scatter_dimension=0, tiled=True).reshape(-1)
    outs = []
    start = 0
    for p in parts:
        size = p.size // seqs
        outs.append(reduced[start : start + size].reshape(p.shape[0] // seqs, p.shape[1]))
        start += size
    slope_full = lax.dynamic_update_slice_in_dim(
        jnp.zeros((heads,), f32), part_slope, tier_pos * hpt, 0
    )
    gain_total, slope_total = lax.psum((part_gain, slope_full), ("seq", "tier"))
    return (
        output[None],
        grad_input[None],
        hidden_own[None],
        new_compressed[None],
        outs[0],
        outs[1],
        outs[2],
        outs[3],
        outs[4],
        outs[5],
        outs[6],
        gain_total,
        slope_total,
    )


def solution(mesh):
    placed = (
        P("seq", "tier", None),
        P("seq", "tier", None),
        P("seq", "tier", None),
        P("seq"),
        P("seq"),
        P(),
        P(),
        P(),
        P(),
        P(),
        P(),
        P(),
        P(),
        P(),
        P("seq", "tier", None),
    )
    return jax.shard_map(
        per_device,
        mesh=mesh,
        in_specs=placed,
        out_specs=(
            P("seq", "tier", None),
            P("seq", "tier", None),
            P("seq", "tier", None),
            P("seq", "tier", None),
            P("seq", "tier"),
            P("seq", "tier"),
            P("seq", "tier"),
            P("seq", "tier"),
            P("seq", "tier"),
            P("seq", "tier"),
            P("seq", "tier"),
            P(),
            P(),
        ),
        check_vma=False,
    )
```

profile of v0, /device:TPU:0, one launch (start us, length us, event | category | flops | bytes accessed | tf_op | source)
XLA Modules:
  0.0 487.0 jit_solution(13463608105993968197)
XLA Ops:
  12.6 3.1 fusion.52
  19.5 23.7 %all-gather.5.cloned.1.call-done = bf16[3,512,1024]{2,1,0:T(8,128)(2,1)} async-done(((bf16[3,128,1024]{2,1,0:T(8,128)(2,1)}), bf16[3,512,1024]{2,1,0:T(8,128)(2,1)}) %all-gather.5.cloned.1.call-update) | async-done | bytes 3145744 | tf_op jit(solution)/shard_map/all_gather | solution.py:80
  43.2 3.7 convolution_convert_fusion
  47.1 2.8 convolution_convert_fusion.5
  57.4 3.4 all-to-all-start
  63.2 2.9 reshape.323
  66.1 4.5 convolution_convert_fusion.2
  82.4 3.1 fusion.54
  92.8 2.6 fusion.93
  98.0 6.0 %fusion.167 = f32[128,4096]{1,0:T(8,128)} fusion(bf16[1024,4096]{1,0:T(8,128)(2,1)} %param.24, f32[128,1024]{1,0:T(8,128)S(1)} %get-tuple-element.44, f32[1024]{0:T(1024)S(1)} %copy-done.38, f32[128]{0:T(128)S(1)} %fusion.135, f32[128]{0:T(128)S(1)} %broadcast_multiply_fusion), kind=kOutput, calls=%fused_computation.219 | convolution fusion | flops 1074266112 | bytes 11015168 | tf_op jit(solution)/shard_map/dot_general | solution.py:30
  104.0 13.6 %multiply_reduce_fusion.4 = (f32[1024]{0:T(1024)S(1)}, f32[128]{0:T(128)S(1)}, f32[128,1024]{1,0:T(8,128)}) fusion(f32[128,1024]{1,0:T(8,128)S(1)} %get-tuple-element.44, f32[128]{0:T(128)S(1)} %fusion.135, f32[128]{0:T(128)S(1)} %broadcast_multiply_fusion, f32[1024]{0:T(1024)S(1)} %copy-done.38, bf16[1024,4096]{1,0:T(8,128)(2,1)} %param.24, ...), kind=kOutput, calls=%fused_computation.135 | convolution fusion | flops 2159279104 | bytes 20195328 | tf_op jit(solution)/shard_map/dot_general | solution.py:38
  123.5 3.5 all-to-all-start.1
  127.1 2.5 fusion.32
  130.7 5.1 %all-to-all-done.1 = bf16[2,128,1024]{1,0,2:T(2,128)(2,1)S(1)} async-done(((bf16[2,128,1024]{1,0,2:T(2,128)(2,1)}), bf16[2,128,1024]{1,0,2:T(2,128)(2,1)S(1)}, u32[]{:S(2)}, u32[]{:S(2)}) %all-to-all-start.1) | async-done | bytes 524320 | tf_op jit(solution)/shard_map/all_to_all | solution.py:159
  137.0 4.9 %multiply_reduce_fusion.1 = (f32[2,512]{1,0:T(2,128)S(1)}, f32[2,512,1536]{2,1,0:T(8,128)S(1)}) fusion(f32[2,512,1536]{2,1,0:T(8,128)} %copy-done.2, f32[2,512]{1,0:T(2,128)S(1)} %log_add_fusion, bf16[512,2,128]{0,2,1:T(8,128)(2,1)S(1)} %reshape.348, bf16[1536,2,128]{0,2,1:T(8,128)(2,1)S(1)} %bitcast.169), kind=kOutput, calls=%fused_computation.13 | convolution fusion | flops 407370752 | bytes 13639680 | tf_op jit(solution)/shard_map/rhd,khd->hrk/dot_general | solution.py:179
  141.9 4.7 multiply_reduce_fusion
  152.6 2.6 fusion.17
  157.8 4.2 convolution_convert_fusion.1
  171.1 3.2 fusion.117
  174.3 4.8 reshape.333
  183.8 7.3 %fusion.63 = f32[512,4096]{1,0:T(8,128)S(1)} fusion(bf16[1024,4096]{1,0:T(8,128)(2,1)} %param.24, bf16[2,512,1024]{2,1,0:T(8,128)(2,1)} %all-gather.7.cloned.1.call-done), kind=kOutput, calls=%fused_computation.98 | convolution fusion | flops 4294967296 | bytes 17825792 | tf_op jit(solution)/shard_map/dot_general | solution.py:30
  191.1 3.3 copy-done.41
  194.4 4.8 fusion.11
  199.2 5.2 %reshape.328 = f32[8,128,1024]{2,1,0:T(8,128)} reshape(f32[4096,256]{1,0:T(8,128)} %fusion.11) | data formatting | bytes 8388608 | tf_op jit(solution)/shard_map/reshape | solution.py:204
  205.5 7.7 %convolution_dynamic-update-slice_fusion = f32[8,480,1024]{2,1,0:T(8,128)} fusion(f32[8,480,1024]{2,1,0:T(8,128)} %constant_dynamic-update-slice_fusion.2, bf16[8,128,512]{2,1,0:T(8,128)(2,1)} %bitcast.187, f32[512,4096]{1,0:T(8,128)} %copy-done.41, s32[]{:T(128)S(6)} %select_n.37, bf16[512,1024]{1,0:T(8,128)(2,1)S(1)} %copy-done.24, ...), kind=kOutput, calls=%fused_computation.30 | convolution fusion | flops 2157969408 | bytes 10486784 | tf_op jit(solution)/shard_map/dot_general | solution.py:34
  213.2 4.9 %constant_dynamic-update-slice_fusion.1 = f32[8,480,1024]{2,1,0:T(8,128)} fusion(f32[8,480,1024]{2,1,0:T(8,128)} %convolution_dynamic-update-slice_fusion, f32[8,128,1024]{2,1,0:T(8,128)} %reshape.328), kind=kLoop, calls=%fused_computation.164 | loop fusion | bytes 8388608
  224.7 2.8 pad_maximum_fusion.1
  227.5 3.5 all-to-all-start.2
  231.0 6.3 %fusion.56 = bf16[1,128,1024]{2,1,0:T(8,128)(2,1)} fusion(f32[128,1024]{1,0:T(8,128)S(1)} %get-tuple-element.44, bf16[4096,1024]{1,0:T(8,128)(2,1)} %param.25, f32[128,4096]{1,0:T(8,128)} %fusion.167, f32[128]{0:T(128)S(1)} %compare_convert_fusion), kind=kOutput, calls=%fused_computation.83 | convolution fusion | flops 1078853632 | bytes 11272704 | tf_op jit(solution)/shard_map/dot_general | solution.py:30
  237.4 47.4 %all-reduce.1 = (f32[1024]{0:T(1024)}, f32[8]{0:T(128)}) all-reduce(f32[1024]{0:T(1024)S(1)} %get-tuple-element.13, f32[8]{0:T(128)S(1)} %negate_dynamic-update-slice_fusion), channel_id=1, replica_groups=mesh['seq'=8,'tier'=4] {'seq','tier'}, use_global_device_ids=true, to_apply=%region_15.16 | all-reduce | flops 1032 | bytes 8256 | tf_op jit(solution)/shard_map/psum | solution.py:216
  285.5 2.9 convolution_add_fusion.2
  292.5 179.6 %reduce-scatter.5.cloned.1.call-done = f32[480,1024]{1,0:T(8,128)} async-done(((f32[3840,1024]{1,0:T(8,128)}), f32[480,1024]{1,0:T(8,128)}) %reduce-scatter.5.cloned.1.call-update) | async-done | bytes 1966096 | tf_op jit(solution)/shard_map/reduce_scatter | solution.py:206
  (194 shorter events, 90.0 us)
Async XLA Ops:
  7.2 89.0 %copy-start = (bf16[1024,1024]{1,0:T(8,128)(2,1)S(1)}, bf16[1024,1024]{1,0:T(8,128)(2,1)}, u32[]{:S(2)}) copy-start(bf16[1024,1024]{1,0:T(8,128)(2,1)} %param.23) | copy-start | bytes 6291460
  7.2 36.0 %all-gather.5.cloned.1.call-start = ((), (), s32[]{:S(2)}) async-start(), calls=%async_computation.5 | async-start | bytes 3932160 | tf_op jit(solution)/shard_map/all_gather | solution.py:80
  11.8 115.3 %all-gather.9.cloned.1.call-start = ((), (), s32[]{:S(2)}) async-start(), calls=%async_computation.9 | async-start | bytes 1310720 | tf_op jit(solution)/shard_map/all_gather | solution.py:81
  19.5 23.7 %copy-start.33 = (bf16[1024,256]{1,0:T(8,128)(2,1)}, bf16[1024,256]{1,0:T(8,128)(2,1)S(1)}, u32[]{:S(2)}) copy-start(bf16[1024,256]{1,0:T(8,128)(2,1)S(1)} %get-tuple-element.53) | copy-start | bytes 1572868
  19.5 27.4 %copy-start.31 = (bf16[1024,256]{1,0:T(8,128)(2,1)}, bf16[1024,256]{1,0:T(8,128)(2,1)S(1)}, u32[]{:S(2)}) copy-start(bf16[1024,256]{1,0:T(8,128)(2,1)S(1)} %get-tuple-element.52) | copy-start | bytes 1572868
  47.1 6.6 %copy-start.7 = (bf16[1536,256]{0,1:T(8,128)(2,1)}, bf16[1536,256]{0,1:T(8,128)(2,1)S(1)}, u32[]{:S(2)}) copy-start(bf16[1536,256]{0,1:T(8,128)(2,1)S(1)} %get-tuple-element.30) | copy-start | bytes 2359300
  57.4 38.1 %all-to-all-start = ((bf16[4,128,256]{1,2,0:T(8,128)(2,1)}), bf16[4,128,256]{1,2,0:T(8,128)(2,1)S(1)}, u32[]{:S(2)}, u32[]{:S(2)}) async-start(bf16[4,128,256]{1,2,0:T(8,128)(2,1)} %copy.122), calls=%async_computation | async-start | bytes 524288 | tf_op jit(solution)/shard_map/all_to_all | solution.py:111
  60.8 110.3 %reduce-scatter.3.cloned.1.call-start = ((), (), s32[]{:S(2)}) async-start(), calls=%async_computation.7 | async-start | bytes 901120 | tf_op jit(solution)/shard_map/reduce_scatter | solution.py:136
  66.1 4.5 copy-start.32
  66.1 4.5 copy-start.34
  66.1 7.5 %copy-start.29 = (bf16[512,256]{0,1:T(8,128)(2,1)S(1)}, bf16[512,256]{0,1:T(8,128)(2,1)}, u32[]{:S(2)}) copy-start(bf16[512,256]{0,1:T(8,128)(2,1)} %copy-done.28) | copy-start | bytes 786436
  92.8 5.1 %copy-start.38 = (f32[1024]{0:T(1024)S(1)}, f32[1024]{0:T(1024)}, u32[]{:S(2)}) copy-start(f32[1024]{0:T(1024)} %param.26) | copy-start | bytes 12292
  122.4 7.3 %copy-start.21 = (bf16[4,128,256]{1,2,0:T(8,128)(2,1)S(1)}, bf16[4,128,256]{1,2,0:T(8,128)(2,1)}, u32[]{:S(2)}) copy-start(bf16[4,128,256]{1,2,0:T(8,128)(2,1)} %copy-done.20) | copy-start | bytes 786436
  122.4 7.4 %copy-start.27 = (bf16[1,128,1024]{2,1,0:T(8,128)(2,1)S(1)}, bf16[1,128,1024]{2,1,0:T(8,128)(2,1)}, u32[]{:S(2)}) copy-start(bf16[1,128,1024]{2,1,0:T(8,128)(2,1)} %get-tuple-element.34) | copy-start | bytes 786436
  123.5 12.3 %all-to-all-start.1 = ((bf16[2,128,1024]{1,0,2:T(2,128)(2,1)}), bf16[2,128,1024]{1,0,2:T(2,128)(2,1)S(1)}, u32[]{:S(2)}, u32[]{:S(2)}) async-start(bf16[2,128,1024]{1,0,2:T(2,128)(2,1)} %copy.123), calls=%async_computation.1 | async-start | bytes 1048576 | tf_op jit(solution)/shard_map/all_to_all | solution.py:159
  127.0 52.1 %all-gather.7.cloned.1.call-start = ((), (), s32[]{:S(2)}) async-start(), calls=%async_computation.6 | async-start | bytes 2621440 | tf_op jit(solution)/shard_map/all_gather | solution.py:162
  129.6 7.4 %copy-start.8 = (bf16[1536,256]{0,1:T(8,128)(2,1)S(1)}, bf16[1536,256]{0,1:T(8,128)(2,1)}, u32[]{:S(2)}) copy-start(bf16[1536,256]{0,1:T(8,128)(2,1)} %copy-done.7) | copy-start | bytes 2359300
  130.6 341.4 %reduce-scatter.5.cloned.1.call-start = ((), (), s32[]{:S(2)}) async-start(), calls=%async_computation.8 | async-start | bytes 17694720 | tf_op jit(solution)/shard_map/reduce_scatter | solution.py:206
  137.0 4.9 %copy-start.4 = (f32[1536,512]{0,1:T(8,128)S(1)}, f32[1536,512]{0,1:T(8,128)}, u32[]{:S(2)}) copy-start(f32[1536,512]{0,1:T(8,128)} %get-tuple-element.39) | copy-start | bytes 9437188
  149.4 5.8 %copy-start.18 = (bf16[2,128,512]{2,1,0:T(8,128)(2,1)}, bf16[2,128,512]{2,1,0:T(8,128)(2,1)S(1)}, u32[]{:S(2)}) copy-start(bf16[2,128,512]{2,1,0:T(8,128)(2,1)S(1)} %fusion.50) | copy-start | bytes 786436
  165.2 4.8 copy-start.12
  165.2 5.9 %copy-start.11 = (bf16[171,3072]{1,0:T(8,128)(2,1)S(1)}, bf16[171,3072]{1,0:T(8,128)(2,1)}, u32[]{:S(2)}) copy-start(bf16[171,3072]{1,0:T(8,128)(2,1)} %reshape.323) | copy-start | bytes 3151876
  174.3 4.9 copy-start.37
  183.8 10.6 %copy-start.24 = (bf16[512,1024]{1,0:T(8,128)(2,1)S(1)}, bf16[512,1024]{1,0:T(8,128)(2,1)}, u32[]{:S(2)}) copy-start(bf16[512,1024]{1,0:T(8,128)(2,1)} %fusion.32) | copy-start | bytes 3145732
  213.2 4.9 %copy-start.5 = (f32[8,96,1024]{2,1,0:T(8,128)S(1)}, f32[8,96,1024]{2,1,0:T(8,128)}, u32[]{:S(2)}) copy-start(f32[8,96,1024]{2,1,0:T(8,128)} %reshape.333) | copy-start | bytes 9437188
  219.9 4.3 copy-start.19
  227.5 57.3 %all-to-all-start.2 = ((bf16[3,512,256]{2,0,1:T(4,128)(2,1)}), bf16[3,512,256]{2,0,1:T(4,128)(2,1)S(1)}, u32[]{:S(2)}, u32[]{:S(2)}) async-start(bf16[3,512,256]{2,0,1:T(4,128)(2,1)} %pad_maximum_fusion.1), calls=%async_computation.2 | async-start | bytes 2097152 | tf_op jit(solution)/shard_map/all_to_all | solution.py:198
  237.3 48.2 %copy-start.10 = (f32[128,1024]{1,0:T(8,128)S(1)}, f32[128,1024]{1,0:T(8,128)}, u32[]{:S(2)}) copy-start(f32[128,1024]{1,0:T(8,128)} %copy-done.9) | copy-start | bytes 1572868
  237.3 48.2 %copy-start.22 = (bf16[1,128,1024]{2,1,0:T(8,128)(2,1)S(1)}, bf16[1,128,1024]{2,1,0:T(8,128)(2,1)}, u32[]{:S(2)}) copy-start(bf16[1,128,1024]{2,1,0:T(8,128)(2,1)} %param.29) | copy-start | bytes 786436
  285.5 5.3 %copy-start.13 = (bf16[1024,1024]{1,0:T(8,128)(2,1)S(1)}, bf16[1024,1024]{1,0:T(8,128)(2,1)}, u32[]{:S(2)}) copy-start(bf16[1024,1024]{1,0:T(8,128)(2,1)} %param.22) | copy-start | bytes 6291460
  472.1 7.1 %slice-start = ((f32[480,1024]{1,0:T(8,128)}), f32[96,1024]{1,0:T(8,128)S(1)}, s32[]{:S(2)}) async-start(f32[480,1024]{1,0:T(8,128)} %reduce-scatter.5.cloned.1.call-done), calls=%async_computation.10 | async-start | bytes 786432 | tf_op jit(solution)/shard_map/slice | solution.py:211
  472.1 7.9 %copy-start.1 = (bf16[1024,1024]{1,0:T(8,128)(2,1)S(1)}, bf16[1024,1024]{1,0:T(8,128)(2,1)}, u32[]{:S(2)}) copy-start(bf16[1024,1024]{1,0:T(8,128)(2,1)} %param.23) | copy-start | bytes 6291460
  (19 other events, 46.1 us)
Sparse Core Ops, SparseCore 0:
  12.0 31.2 all-gather.4
  44.8 16.7 all-gather.8
  95.6 24.2 reduce-scatter.2
  130.8 23.9 all-gather.6
  220.1 251.9 reduce-scatter.4
where the time goes:
time: 495 us; the launch traced here: 487 us
  waiting for transfers between devices  209 us (42%)
  matrix products  110 us (22%)
  local copies, waits for them, and re-layouts  69.5 us (14%)
  blocking collectives  47.4 us (10%)
  other arithmetic  24.3 us (5%)
  between operations  16.5 us (3%)
  starting transfers between devices  10.6 us (2%)
    reduce_scatter x1, waiting for transfers between devices, per_device(): lax.psum_scatter(flat, 'seq', scatter_dimension=0, tiled=True).reshape(-1)  180 us
    psum x1, blocking collectives, per_device(): gain_total, slope_total = lax.psum((part_gain, slope_full), ('seq', 'tier'))  47.4 us
    dot_general x8, matrix products, mm(): return jnp.dot(left, right, preferred_element_type=f32)  32.5 us
    dot_general x6, matrix products, mm_nt(): lax.dot_general(left, right, (((1,), (1,)), ((), ())), preferred_element_...  24 us
    all_gather x1, waiting for transfers between devices, per_device(): raw_seq = lax.all_gather(raw_local, 'tier', axis=1, tiled=True)  23.7 us
    unnamed x93, local copies, waits for them, and re-layouts  22 us
    dot_general x7, matrix products, mm_tn(): lax.dot_general(left, right, (((0,), (0,)), ((), ())), preferred_element_...  21.3 us
    reshape x6, local copies, waits for them, and re-layouts, per_device(): flat = jnp.concatenate([p.reshape(seqs, -1, width) for p in parts], axis=1)  14.1 us
  transfers between devices with their start and end apart: 8, of which 3 were waited for; matrix products, arithmetic and copies ran while one was open for 30% of the time, Pallas kernels for 0%

commit v1 on v0

--- a/solution.py
+++ b/solution.py
@@ -213,7 +213,7 @@
     slope_full = lax.dynamic_update_slice_in_dim(
         jnp.zeros((heads,), f32), part_slope, tier_pos * hpt, 0
     )
-    gain_total, slope_total = lax.psum((part_gain, slope_full), ("seq", "tier"))
+    gain_total, slope_total = lax.psum(lax.psum((part_gain, slope_full), "tier"), "seq")
     return (
         output[None],
         grad_input[None],

time: 495 us -> 495 us (level)
  waiting for transfers between devices: 209 us -> 223 us
  blocking collectives: 47.4 us -> 33.9 us
    psum x1 -> x2, blocking collectives: 47.4 us -> 33.9 us  [the longest x1 24.2 us: per_device(): lax.psum(lax.psum((part_gain, slope_full), 'tier'), 'seq')]
    reduce_scatter x1, waiting for transfers between devices: 180 us -> 193 us  [per_device(): lax.psum_scatter(flat, 'seq', scatter_dimension=0, tiled=True).reshape(-1)]
where the time goes in v1:
time: 495 us; the launch traced here: 487 us
  waiting for transfers between devices  223 us (45%)
  matrix products  109 us (22%)
  local copies, waits for them, and re-layouts  69.5 us (14%)
  blocking collectives  33.9 us (7%)
  other arithmetic  24.3 us (5%)
  between operations  16.5 us (3%)
  starting transfers between devices  10.6 us (2%)
    reduce_scatter x1, waiting for transfers between devices, per_device(): lax.psum_scatter(flat, 'seq', scatter_dimension=0, tiled=True).reshape(-1)  193 us
    dot_general x8, matrix products, mm(): return jnp.dot(left, right, preferred_element_type=f32)  32.5 us
    psum x1, blocking collectives, per_device(): lax.psum(lax.psum((part_gain, slope_full), 'tier'), 'seq')  24.2 us
    dot_general x6, matrix products, mm_nt(): lax.dot_general(left, right, (((1,), (1,)), ((), ())), preferred_element_...  23.7 us
    all_gather x1, waiting for transfers between devices, per_device(): raw_seq = lax.all_gather(raw_local, 'tier', axis=1, tiled=True)  23.7 us
    unnamed x93, local copies, waits for them, and re-layouts  22.1 us
    dot_general x7, matrix products, mm_tn(): lax.dot_general(left, right, (((0,), (0,)), ((), ())), preferred_element_...  21.3 us
    reshape x6, local copies, waits for them, and re-layouts, per_device(): flat = jnp.concatenate([p.reshape(seqs, -1, width) for p in parts], axis=1)  14.1 us
  transfers between devices with their start and end apart: 8, of which 3 were waited for; matrix products, arithmetic and copies ran while one was open for 30% of the time, Pallas kernels for 0%

profile of v1, /device:TPU:0, one launch (start us, length us, event | category | flops | bytes accessed | tf_op | source)
XLA Modules:
  0.0 486.6 jit_solution(12790255855068029225)
XLA Ops:
  12.6 3.1 fusion.52
  19.5 23.7 %all-gather.5.cloned.1.call-done = bf16[3,512,1024]{2,1,0:T(8,128)(2,1)} async-done(((bf16[3,128,1024]{2,1,0:T(8,128)(2,1)}), bf16[3,512,1024]{2,1,0:T(8,128)(2,1)}) %all-gather.5.cloned.1.call-update) | async-done | bytes 3145744 | tf_op jit(solution)/shard_map/all_gather | solution.py:80
  43.3 3.7 convolution_convert_fusion
  47.1 2.8 convolution_convert_fusion.5
  57.4 3.4 all-to-all-start
  63.2 2.9 reshape.323
  66.1 4.5 convolution_convert_fusion.2
  82.4 3.1 fusion.54
  92.9 2.6 fusion.93
  98.1 6.0 %fusion.167 = f32[128,4096]{1,0:T(8,128)} fusion(bf16[1024,4096]{1,0:T(8,128)(2,1)} %param.24, f32[128,1024]{1,0:T(8,128)S(1)} %get-tuple-element.46, f32[1024]{0:T(1024)S(1)} %copy-done.38, f32[128]{0:T(128)S(1)} %fusion.135, f32[128]{0:T(128)S(1)} %broadcast_multiply_fusion), kind=kOutput, calls=%fused_computation.219 | convolution fusion | flops 1074266112 | bytes 11015168 | tf_op jit(solution)/shard_map/dot_general | solution.py:30
  104.1 13.6 %multiply_reduce_fusion.4 = (f32[1024]{0:T(1024)S(1)}, f32[128]{0:T(128)S(1)}, f32[128,1024]{1,0:T(8,128)}) fusion(f32[128,1024]{1,0:T(8,128)S(1)} %get-tuple-element.46, f32[128]{0:T(128)S(1)} %fusion.135, f32[128]{0:T(128)S(1)} %broadcast_multiply_fusion, f32[1024]{0:T(1024)S(1)} %copy-done.38, bf16[1024,4096]{1,0:T(8,128)(2,1)} %param.24, ...), kind=kOutput, calls=%fused_computation.135 | convolution fusion | flops 2159279104 | bytes 20195328 | tf_op jit(solution)/shard_map/dot_general | solution.py:38
  123.6 3.5 all-to-all-start.1
  130.8 5.1 %all-to-all-done.1 = bf16[2,128,1024]{1,0,2:T(2,128)(2,1)S(1)} async-done(((bf16[2,128,1024]{1,0,2:T(2,128)(2,1)}), bf16[2,128,1024]{1,0,2:T(2,128)(2,1)S(1)}, u32[]{:S(2)}, u32[]{:S(2)}) %all-to-all-start.1) | async-done | bytes 524320 | tf_op jit(solution)/shard_map/all_to_all | solution.py:159
  137.1 4.9 %multiply_reduce_fusion.1 = (f32[2,512]{1,0:T(2,128)S(1)}, f32[2,512,1536]{2,1,0:T(8,128)S(1)}) fusion(f32[2,512,1536]{2,1,0:T(8,128)} %copy-done.2, f32[2,512]{1,0:T(2,128)S(1)} %log_add_fusion, bf16[512,2,128]{0,2,1:T(8,128)(2,1)S(1)} %reshape.348, bf16[1536,2,128]{0,2,1:T(8,128)(2,1)S(1)} %bitcast.169), kind=kOutput, calls=%fused_computation.13 | convolution fusion | flops 407370752 | bytes 13639680 | tf_op jit(solution)/shard_map/rhd,khd->hrk/dot_general | solution.py:179
  142.0 4.7 multiply_reduce_fusion
  152.7 2.6 fusion.17
  157.8 4.2 convolution_convert_fusion.1
  171.2 3.2 fusion.117
  174.4 4.8 reshape.333
  183.9 7.3 %fusion.63 = f32[512,4096]{1,0:T(8,128)S(1)} fusion(bf16[1024,4096]{1,0:T(8,128)(2,1)} %param.24, bf16[2,512,1024]{2,1,0:T(8,128)(2,1)} %all-gather.7.cloned.1.call-done), kind=kOutput, calls=%fused_computation.98 | convolution fusion | flops 4294967296 | bytes 17825792 | tf_op jit(solution)/shard_map/dot_general | solution.py:30
  191.2 3.2 copy-done.41
  194.4 4.8 fusion.11
  199.2 5.2 %reshape.328 = f32[8,128,1024]{2,1,0:T(8,128)} reshape(f32[4096,256]{1,0:T(8,128)} %fusion.11) | data formatting | bytes 8388608 | tf_op jit(solution)/shard_map/reshape | solution.py:204
  205.5 7.7 %convolution_dynamic-update-slice_fusion = f32[8,480,1024]{2,1,0:T(8,128)} fusion(f32[8,480,1024]{2,1,0:T(8,128)} %constant_dynamic-update-slice_fusion.2, bf16[8,128,512]{2,1,0:T(8,128)(2,1)} %bitcast.187, f32[512,4096]{1,0:T(8,128)} %copy-done.41, s32[]{:T(128)S(6)} %select_n.37, bf16[512,1024]{1,0:T(8,128)(2,1)S(1)} %copy-done.24, ...), kind=kOutput, calls=%fused_computation.30 | convolution fusion | flops 2157969408 | bytes 10486784 | tf_op jit(solution)/shard_map/dot_general | solution.py:34
  213.2 4.9 %constant_dynamic-update-slice_fusion.1 = f32[8,480,1024]{2,1,0:T(8,128)} fusion(f32[8,480,1024]{2,1,0:T(8,128)} %convolution_dynamic-update-slice_fusion, f32[8,128,1024]{2,1,0:T(8,128)} %reshape.328), kind=kLoop, calls=%fused_computation.164 | loop fusion | bytes 8388608
  224.7 2.8 pad_maximum_fusion.1
  227.5 3.5 all-to-all-start.2
  231.0 6.3 %fusion.56 = bf16[1,128,1024]{2,1,0:T(8,128)(2,1)} fusion(f32[128,1024]{1,0:T(8,128)S(1)} %get-tuple-element.46, bf16[4096,1024]{1,0:T(8,128)(2,1)} %param.25, f32[128,4096]{1,0:T(8,128)} %fusion.167, f32[128]{0:T(128)S(1)} %compare_convert_fusion), kind=kOutput, calls=%fused_computation.83 | convolution fusion | flops 1078853632 | bytes 11272704 | tf_op jit(solution)/shard_map/dot_general | solution.py:30
  237.4 9.8 %all-reduce.2 = (f32[1024]{0:T(1024)S(1)}, f32[8]{0:T(128)S(1)}) all-reduce(f32[1024]{0:T(1024)S(1)} %get-tuple-element.13, f32[8]{0:T(128)S(1)} %negate_dynamic-update-slice_fusion), channel_id=1, replica_groups=mesh['seq'=8,'tier'=4] {'tier'}, use_global_device_ids=true, to_apply=%region_15.16 | all-reduce | flops 1032 | bytes 8256 | tf_op jit(solution)/shard_map/psum | solution.py:216
  247.2 24.2 %all-reduce.1 = (f32[1024]{0:T(1024)}, f32[8]{0:T(128)}) all-reduce(f32[1024]{0:T(1024)S(1)} %get-tuple-element.17, f32[8]{0:T(128)S(1)} %get-tuple-element.18), channel_id=1, replica_groups=mesh['seq'=8,'tier'=4] {'seq'}, use_global_device_ids=true, to_apply=%region_16.17 | all-reduce | flops 1032 | bytes 8256 | tf_op jit(solution)/shard_map/psum | solution.py:216
  272.1 2.6 convolution_add_fusion.2
  278.8 192.9 %reduce-scatter.5.cloned.1.call-done = f32[480,1024]{1,0:T(8,128)} async-done(((f32[3840,1024]{1,0:T(8,128)}), f32[480,1024]{1,0:T(8,128)}) %reduce-scatter.5.cloned.1.call-update) | async-done | bytes 1966096 | tf_op jit(solution)/shard_map/reduce_scatter | solution.py:206
  (195 shorter events, 92.5 us)
Async XLA Ops:
  7.2 89.1 %copy-start = (bf16[1024,1024]{1,0:T(8,128)(2,1)S(1)}, bf16[1024,1024]{1,0:T(8,128)(2,1)}, u32[]{:S(2)}) copy-start(bf16[1024,1024]{1,0:T(8,128)(2,1)} %param.23) | copy-start | bytes 6291460
  7.2 36.1 %all-gather.5.cloned.1.call-start = ((), (), s32[]{:S(2)}) async-start(), calls=%async_computation.5 | async-start | bytes 3932160 | tf_op jit(solution)/shard_map/all_gather | solution.py:80
  11.9 115.3 %all-gather.9.cloned.1.call-start = ((), (), s32[]{:S(2)}) async-start(), calls=%async_computation.9 | async-start | bytes 1310720 | tf_op jit(solution)/shard_map/all_gather | solution.py:81
  19.5 23.7 %copy-start.33 = (bf16[1024,256]{1,0:T(8,128)(2,1)}, bf16[1024,256]{1,0:T(8,128)(2,1)S(1)}, u32[]{:S(2)}) copy-start(bf16[1024,256]{1,0:T(8,128)(2,1)S(1)} %get-tuple-element.55) | copy-start | bytes 1572868
  19.5 27.5 %copy-start.31 = (bf16[1024,256]{1,0:T(8,128)(2,1)}, bf16[1024,256]{1,0:T(8,128)(2,1)S(1)}, u32[]{:S(2)}) copy-start(bf16[1024,256]{1,0:T(8,128)(2,1)S(1)} %get-tuple-element.54) | copy-start | bytes 1572868
  47.1 6.6 %copy-start.7 = (bf16[1536,256]{0,1:T(8,128)(2,1)}, bf16[1536,256]{0,1:T(8,128)(2,1)S(1)}, u32[]{:S(2)}) copy-start(bf16[1536,256]{0,1:T(8,128)(2,1)S(1)} %get-tuple-element.32) | copy-start | bytes 2359300
  57.4 38.1 %all-to-all-start = ((bf16[4,128,256]{1,2,0:T(8,128)(2,1)}), bf16[4,128,256]{1,2,0:T(8,128)(2,1)S(1)}, u32[]{:S(2)}, u32[]{:S(2)}) async-start(bf16[4,128,256]{1,2,0:T(8,128)(2,1)} %copy.122), calls=%async_computation | async-start | bytes 524288 | tf_op jit(solution)/shard_map/all_to_all | solution.py:111
  60.8 110.3 %reduce-scatter.3.cloned.1.call-start = ((), (), s32[]{:S(2)}) async-start(), calls=%async_computation.7 | async-start | bytes 901120 | tf_op jit(solution)/shard_map/reduce_scatter | solution.py:136
  66.1 4.5 copy-start.32
  66.1 4.5 copy-start.34
  66.1 7.5 %copy-start.29 = (bf16[512,256]{0,1:T(8,128)(2,1)S(1)}, bf16[512,256]{0,1:T(8,128)(2,1)}, u32[]{:S(2)}) copy-start(bf16[512,256]{0,1:T(8,128)(2,1)} %copy-done.28) | copy-start | bytes 786436
  92.9 5.2 %copy-start.38 = (f32[1024]{0:T(1024)S(1)}, f32[1024]{0:T(1024)}, u32[]{:S(2)}) copy-start(f32[1024]{0:T(1024)} %param.26) | copy-start | bytes 12292
  122.4 7.3 %copy-start.21 = (bf16[4,128,256]{1,2,0:T(8,128)(2,1)S(1)}, bf16[4,128,256]{1,2,0:T(8,128)(2,1)}, u32[]{:S(2)}) copy-start(bf16[4,128,256]{1,2,0:T(8,128)(2,1)} %copy-done.20) | copy-start | bytes 786436
  122.5 7.4 %copy-start.27 = (bf16[1,128,1024]{2,1,0:T(8,128)(2,1)S(1)}, bf16[1,128,1024]{2,1,0:T(8,128)(2,1)}, u32[]{:S(2)}) copy-start(bf16[1,128,1024]{2,1,0:T(8,128)(2,1)} %get-tuple-element.36) | copy-start | bytes 786436
  123.6 12.3 %all-to-all-start.1 = ((bf16[2,128,1024]{1,0,2:T(2,128)(2,1)}), bf16[2,128,1024]{1,0,2:T(2,128)(2,1)S(1)}, u32[]{:S(2)}, u32[]{:S(2)}) async-start(bf16[2,128,1024]{1,0,2:T(2,128)(2,1)} %copy.123), calls=%async_computation.1 | async-start | bytes 1048576 | tf_op jit(solution)/shard_map/all_to_all | solution.py:159
  127.1 52.1 %all-gather.7.cloned.1.call-start = ((), (), s32[]{:S(2)}) async-start(), calls=%async_computation.6 | async-start | bytes 2621440 | tf_op jit(solution)/shard_map/all_gather | solution.py:162
  129.7 7.4 %copy-start.8 = (bf16[1536,256]{0,1:T(8,128)(2,1)S(1)}, bf16[1536,256]{0,1:T(8,128)(2,1)}, u32[]{:S(2)}) copy-start(bf16[1536,256]{0,1:T(8,128)(2,1)} %copy-done.7) | copy-start | bytes 2359300
  130.7 341.0 %reduce-scatter.5.cloned.1.call-start = ((), (), s32[]{:S(2)}) async-start(), calls=%async_computation.8 | async-start | bytes 17694720 | tf_op jit(solution)/shard_map/reduce_scatter | solution.py:206
  137.1 4.9 %copy-start.4 = (f32[1536,512]{0,1:T(8,128)S(1)}, f32[1536,512]{0,1:T(8,128)}, u32[]{:S(2)}) copy-start(f32[1536,512]{0,1:T(8,128)} %get-tuple-element.41) | copy-start | bytes 9437188
  149.5 5.8 %copy-start.18 = (bf16[2,128,512]{2,1,0:T(8,128)(2,1)}, bf16[2,128,512]{2,1,0:T(8,128)(2,1)S(1)}, u32[]{:S(2)}) copy-start(bf16[2,128,512]{2,1,0:T(8,128)(2,1)S(1)} %fusion.50) | copy-start | bytes 786436
  165.3 4.8 copy-start.12
  165.3 5.9 %copy-start.11 = (bf16[171,3072]{1,0:T(8,128)(2,1)S(1)}, bf16[171,3072]{1,0:T(8,128)(2,1)}, u32[]{:S(2)}) copy-start(bf16[171,3072]{1,0:T(8,128)(2,1)} %reshape.323) | copy-start | bytes 3151876
  174.4 4.8 copy-start.37
  183.9 10.5 %copy-start.24 = (bf16[512,1024]{1,0:T(8,128)(2,1)S(1)}, bf16[512,1024]{1,0:T(8,128)(2,1)}, u32[]{:S(2)}) copy-start(bf16[512,1024]{1,0:T(8,128)(2,1)} %fusion.32) | copy-start | bytes 3145732
  213.2 4.9 %copy-start.5 = (f32[8,96,1024]{2,1,0:T(8,128)S(1)}, f32[8,96,1024]{2,1,0:T(8,128)}, u32[]{:S(2)}) copy-start(f32[8,96,1024]{2,1,0:T(8,128)} %reshape.333) | copy-start | bytes 9437188
  220.0 4.3 copy-start.19
  227.5 43.9 %all-to-all-start.2 = ((bf16[3,512,256]{2,0,1:T(4,128)(2,1)}), bf16[3,512,256]{2,0,1:T(4,128)(2,1)S(1)}, u32[]{:S(2)}, u32[]{:S(2)}) async-start(bf16[3,512,256]{2,0,1:T(4,128)(2,1)} %pad_maximum_fusion.1), calls=%async_computation.2 | async-start | bytes 2097152 | tf_op jit(solution)/shard_map/all_to_all | solution.py:198
  237.3 34.7 %copy-start.10 = (f32[128,1024]{1,0:T(8,128)S(1)}, f32[128,1024]{1,0:T(8,128)}, u32[]{:S(2)}) copy-start(f32[128,1024]{1,0:T(8,128)} %copy-done.9) | copy-start | bytes 1572868
  237.3 34.8 %copy-start.22 = (bf16[1,128,1024]{2,1,0:T(8,128)(2,1)S(1)}, bf16[1,128,1024]{2,1,0:T(8,128)(2,1)}, u32[]{:S(2)}) copy-start(bf16[1,128,1024]{2,1,0:T(8,128)(2,1)} %param.29) | copy-start | bytes 786436
  272.1 5.0 %copy-start.13 = (bf16[1024,1024]{1,0:T(8,128)(2,1)S(1)}, bf16[1024,1024]{1,0:T(8,128)(2,1)}, u32[]{:S(2)}) copy-start(bf16[1024,1024]{1,0:T(8,128)(2,1)} %param.22) | copy-start | bytes 6291460
  471.7 7.1 %slice-start = ((f32[480,1024]{1,0:T(8,128)}), f32[96,1024]{1,0:T(8,128)S(1)}, s32[]{:S(2)}) async-start(f32[480,1024]{1,0:T(8,128)} %reduce-scatter.5.cloned.1.call-done), calls=%async_computation.10 | async-start | bytes 786432 | tf_op jit(solution)/shard_map/slice | solution.py:211
  471.7 7.9 %copy-start.1 = (bf16[1024,1024]{1,0:T(8,128)(2,1)S(1)}, bf16[1024,1024]{1,0:T(8,128)(2,1)}, u32[]{:S(2)}) copy-start(bf16[1024,1024]{1,0:T(8,128)(2,1)} %param.23) | copy-start | bytes 6291460
  (19 other events, 46.1 us)
Sparse Core Ops, SparseCore 0:
  12.0 31.2 all-gather.4
  44.8 16.7 all-gather.8
  95.6 24.2 reduce-scatter.2
  130.9 23.9 all-gather.6
  220.1 251.5 reduce-scatter.4
